TPU v7x, 768 devices: a whole 4x8x12 slice. The times are simulated.
768 devices in a mesh: dp: 192 (over z, y, core), section: 4 (over x).
Axes of the slice: x: 4, y: 8, z: 12, core: 2. Of those that a mesh axis runs over, the one named last changes fastest.
Arguments:
- layer_inputs: bfloat16 [4, 24576, 4096], P('section', 'dp'), may hold values from -6 to 6
- top_grad: bfloat16 [24576, 4096], P('dp'), may hold values from -2.5 to 2.5
- value_grads: bfloat16 [4, 24576, 128], P('section', 'dp'), may hold values from -6 to 6
- weights: bfloat16 [4, 4096, 128], P('section'), may hold values from -0.09375 to 0.09375
- norm_gains: float32 [4, 4096], P('section'), may hold values from 0.5 to 1.5
- counts: int32 [1536], P('dp'), may hold values from 1 to 16, as said below
Outputs:
- input_grads: bfloat16 [4, 24576, 4096], P('section', 'dp')
- weight_grads: float32 [4, 528384], P('section', 'dp')
Inputs may be any that keep to these rules, and one draw needn't show every extreme that they name: Entry m of a device's block of counts belongs to its m-th micro-batch; slots at or past the count are padding. Some micro-batch holds 16 live slots and some holds 1.
All inputs are finite; a program needn't handle non-finite values.
Results may differ from a plain program's by a relative error of at most 0.0034.
Values may be sent and summed in bfloat16 or wider, within the bound.
A program may use at most 32 MiB of HBM per device.

v0:
```python
import math

import jax
import jax.numpy as jnp
from jax import lax
from jax.sharding import PartitionSpec as P

eps_norm = 1e-05


def from_behind(array, axis, by):
    peers = lax.axis_size(axis)
    pairs = [(i, i + by) for i in range(peers) if 0 <= i + by < peers]
    return lax.ppermute(array, axis, pairs)


def run_chain(top_blocks, branch_blocks):
    groups = top_blocks.shape[0]
    section_here = lax.axis_index("section")
    last_section = lax.axis_size("section") - 1
    delay = last_section - section_here

    def advance(counter, carry):
        sent, result = carry
        received = from_behind(sent, "section", -1)
        micro_here = counter - delay
        picked = jnp.clip(micro_here, 0, groups - 1)
        top_piece = lax.dynamic_index_in_dim(top_blocks, picked, 0, keepdims=False)
        branch_piece = lax.dynamic_index_in_dim(branch_blocks, picked, 0, keepdims=False)
        incoming = jnp.where(section_here == last_section, top_piece, received)
        updated = (incoming.astype(jnp.float32) + branch_piece).astype(jnp.bfloat16)
        usable = (micro_here >= 0) & (micro_here < groups)
        current = lax.dynamic_index_in_dim(result, picked, 0, keepdims=False)
        result = lax.dynamic_update_index_in_dim(
            result, jnp.where(usable, updated, current), picked, 0
        )
        return (updated, result)

    start = (jnp.zeros(top_blocks.shape[1:], jnp.bfloat16), jnp.zeros_like(top_blocks))
    final_pair = lax.fori_loop(0, groups + last_section, advance, start)
    return final_pair[1]


def weight_owned(unit, back, normed, masked, factor):
    weight_term = lax.dot_general(
        normed, masked, (((0,), (0,)), ((), ())), preferred_element_type=jnp.float32
    )
    gain_term = jnp.sum(unit * back, axis=0)
    packed_terms = jnp.concatenate([gain_term, weight_term.reshape(-1)]) * factor
    return lax.psum_scatter(packed_terms, "dp", scatter_dimension=0, tiled=True)


def shards(layer_inputs, top_grad, value_grads, weights, norm_gains, counts):
    row_count = layer_inputs.shape[1]
    width = layer_inputs.shape[2]
    micro_count = counts.shape[0]
    slots = row_count // micro_count
    slot_index = jnp.arange(slots, dtype=jnp.int32)
    live = (slot_index[None, :] < counts[:, None]).reshape(row_count)
    factor = 1.0 / math.sqrt(row_count * lax.axis_size("dp"))
    inputs_wide = layer_inputs[0].astype(jnp.float32)
    scale = lax.rsqrt(jnp.mean(inputs_wide * inputs_wide, axis=1, keepdims=True) + eps_norm)
    unit = inputs_wide * scale
    gain_row = norm_gains[0]
    normed = (unit * gain_row).astype(jnp.bfloat16)
    masked = jnp.where(live[:, None], value_grads[0], jnp.zeros((), value_grads.dtype))
    back = lax.dot_general(
        masked, weights[0], (((1,), (1,)), ((), ())), preferred_element_type=jnp.float32
    )
    branch = scale * (
        gain_row * back - unit * jnp.mean(unit * gain_row * back, axis=1, keepdims=True)
    )
    group_size = 1
    top_blocks = top_grad.reshape(micro_count // group_size, group_size * slots, width)
    branch_blocks = branch.reshape(micro_count // group_size, group_size * slots, width)
    owned = weight_owned(unit, back, normed, masked, factor)
    chained = run_chain(top_blocks, branch_blocks)
    return (chained.reshape(1, row_count, width), owned[None, :])


def solution(mesh):
    placed = (
        P("section", "dp", None),
        P("dp", None),
        P("section", "dp", None),
        P("section", None, None),
        P("section", None),
        P("dp"),
    )
    return jax.shard_map(
        shards,
        mesh=mesh,
        in_specs=placed,
        out_specs=(P("section", "dp", None), P("section", "dp")),
        check_vma=False,
    )
```

profile of v0, /device:TPU:26, one launch (start us, length us, event | category | flops | bytes accessed | tf_op | source)
XLA Modules:
  0.0 432.6 jit_solution(16096229153115921176)
XLA Ops:
  7.2 0.0 all-reduce.3.cloned.1.call-start
  7.3 1.7 fusion.11
  8.9 0.7 iota_compare_fusion
  9.7 0.1 lt.48
  9.7 1.8 convolution_bitcast_fusion
  11.6 2.0 fusion.10
  13.6 1.5 maximum_multiply_fusion
  15.1 1.3 dynamic-slice
  17.0 3.4 fusion.9
  20.4 313.3 %all-reduce.3.cloned.1.call-done = f32[528384]{0:T(1024)} async-done(((f32[528384]{0:T(1024)}), f32[528384]{0:T(1024)}) %all-reduce.3.cloned.1.call-update) | async-done | bytes 2113552
  333.8 0.8 dynamic-slice.1
  334.6 0.6 broadcast_in_dim.39
  335.2 0.1 broadcast_in_dim.36
  335.3 89.5 %while.18 = (s32[]{:T(128)}, bf16[16,4096]{1,0:T(8,128)(2,1)S(1)}, bf16[8,16,4096]{2,1,0:T(8,128)(2,1)S(1)}, pred[]{:T(512)}, s32[]{:T(128)}, /*index=5*/bf16[8,...) while((s32[]{:T(128)}, bf16[16,4096]{1,0:T(8,128)(2,1)S(1)}, ...), condition=%wide.region_3.4_spmd.clone, body=%wide.region_2.3_spmd.clone.sunk | while | flops 393225 | bytes 1966306 | solution.py:40
  335.3 2.5 collective-permute-start
  337.8 4.3 %collective-permute-done = bf16[16,4096]{1,0:T(8,128)(2,1)S(1)} collective-permute-done((bf16[16,4096]{1,0:T(8,128)(2,1)S(1)}, bf16[16,4096]{1,0:T(8,128)(2,1)S(1)}, u32[]{:S(2)}, u32[]{:S(2)}) %collective-permute-start) | collective-permute-done | bytes 131104 | tf_op jit(solution)/shard_map/while/body/eval_jaxpr/ppermute | solution.py:14
  342.2 1.0 bitcast_dynamic-update-slice_fusion.2
  343.3 2.5 collective-permute-start
  345.8 4.3 %collective-permute-done = bf16[16,4096]{1,0:T(8,128)(2,1)S(1)} collective-permute-done((bf16[16,4096]{1,0:T(8,128)(2,1)S(1)}, bf16[16,4096]{1,0:T(8,128)(2,1)S(1)}, u32[]{:S(2)}, u32[]{:S(2)}) %collective-permute-start) | collective-permute-done | bytes 131104 | tf_op jit(solution)/shard_map/while/body/eval_jaxpr/ppermute | solution.py:14
  350.1 1.0 bitcast_dynamic-update-slice_fusion.2
  351.2 2.5 collective-permute-start
  353.7 4.3 %collective-permute-done = bf16[16,4096]{1,0:T(8,128)(2,1)S(1)} collective-permute-done((bf16[16,4096]{1,0:T(8,128)(2,1)S(1)}, bf16[16,4096]{1,0:T(8,128)(2,1)S(1)}, u32[]{:S(2)}, u32[]{:S(2)}) %collective-permute-start) | collective-permute-done | bytes 131104 | tf_op jit(solution)/shard_map/while/body/eval_jaxpr/ppermute | solution.py:14
  358.1 1.0 bitcast_dynamic-update-slice_fusion.2
  359.2 2.5 collective-permute-start
  361.7 4.8 %collective-permute-done = bf16[16,4096]{1,0:T(8,128)(2,1)S(1)} collective-permute-done((bf16[16,4096]{1,0:T(8,128)(2,1)S(1)}, bf16[16,4096]{1,0:T(8,128)(2,1)S(1)}, u32[]{:S(2)}, u32[]{:S(2)}) %collective-permute-start) | collective-permute-done | bytes 131104 | tf_op jit(solution)/shard_map/while/body/eval_jaxpr/ppermute | solution.py:14
  366.5 1.0 bitcast_dynamic-update-slice_fusion.2
  367.6 2.5 collective-permute-start
  370.1 5.6 %collective-permute-done = bf16[16,4096]{1,0:T(8,128)(2,1)S(1)} collective-permute-done((bf16[16,4096]{1,0:T(8,128)(2,1)S(1)}, bf16[16,4096]{1,0:T(8,128)(2,1)S(1)}, u32[]{:S(2)}, u32[]{:S(2)}) %collective-permute-start) | collective-permute-done | bytes 131104 | tf_op jit(solution)/shard_map/while/body/eval_jaxpr/ppermute | solution.py:14
  375.6 1.0 bitcast_dynamic-update-slice_fusion.2
  376.7 2.5 collective-permute-start
  379.2 4.7 %collective-permute-done = bf16[16,4096]{1,0:T(8,128)(2,1)S(1)} collective-permute-done((bf16[16,4096]{1,0:T(8,128)(2,1)S(1)}, bf16[16,4096]{1,0:T(8,128)(2,1)S(1)}, u32[]{:S(2)}, u32[]{:S(2)}) %collective-permute-start) | collective-permute-done | bytes 131104 | tf_op jit(solution)/shard_map/while/body/eval_jaxpr/ppermute | solution.py:14
  383.9 1.0 bitcast_dynamic-update-slice_fusion.2
  385.0 2.5 collective-permute-start
  387.6 4.3 %collective-permute-done = bf16[16,4096]{1,0:T(8,128)(2,1)S(1)} collective-permute-done((bf16[16,4096]{1,0:T(8,128)(2,1)S(1)}, bf16[16,4096]{1,0:T(8,128)(2,1)S(1)}, u32[]{:S(2)}, u32[]{:S(2)}) %collective-permute-start) | collective-permute-done | bytes 131104 | tf_op jit(solution)/shard_map/while/body/eval_jaxpr/ppermute | solution.py:14
  391.9 1.0 bitcast_dynamic-update-slice_fusion.2
  393.0 2.5 collective-permute-start
  395.5 4.3 %collective-permute-done = bf16[16,4096]{1,0:T(8,128)(2,1)S(1)} collective-permute-done((bf16[16,4096]{1,0:T(8,128)(2,1)S(1)}, bf16[16,4096]{1,0:T(8,128)(2,1)S(1)}, u32[]{:S(2)}, u32[]{:S(2)}) %collective-permute-start) | collective-permute-done | bytes 131104 | tf_op jit(solution)/shard_map/while/body/eval_jaxpr/ppermute | solution.py:14
  399.9 1.0 bitcast_dynamic-update-slice_fusion.2
  400.9 2.5 collective-permute-start
  403.5 4.3 %collective-permute-done = bf16[16,4096]{1,0:T(8,128)(2,1)S(1)} collective-permute-done((bf16[16,4096]{1,0:T(8,128)(2,1)S(1)}, bf16[16,4096]{1,0:T(8,128)(2,1)S(1)}, u32[]{:S(2)}, u32[]{:S(2)}) %collective-permute-start) | collective-permute-done | bytes 131104 | tf_op jit(solution)/shard_map/while/body/eval_jaxpr/ppermute | solution.py:14
  407.8 1.0 bitcast_dynamic-update-slice_fusion.2
  408.9 2.5 collective-permute-start
  411.4 4.3 %collective-permute-done = bf16[16,4096]{1,0:T(8,128)(2,1)S(1)} collective-permute-done((bf16[16,4096]{1,0:T(8,128)(2,1)S(1)}, bf16[16,4096]{1,0:T(8,128)(2,1)S(1)}, u32[]{:S(2)}, u32[]{:S(2)}) %collective-permute-start) | collective-permute-done | bytes 131104 | tf_op jit(solution)/shard_map/while/body/eval_jaxpr/ppermute | solution.py:14
  415.8 1.0 bitcast_dynamic-update-slice_fusion.2
  416.8 2.5 collective-permute-start
  419.4 4.3 %collective-permute-done = bf16[16,4096]{1,0:T(8,128)(2,1)S(1)} collective-permute-done((bf16[16,4096]{1,0:T(8,128)(2,1)S(1)}, bf16[16,4096]{1,0:T(8,128)(2,1)S(1)}, u32[]{:S(2)}, u32[]{:S(2)}) %collective-permute-start) | collective-permute-done | bytes 131104 | tf_op jit(solution)/shard_map/while/body/eval_jaxpr/ppermute | solution.py:14
  423.7 1.0 bitcast_dynamic-update-slice_fusion.2
  424.8 1.0 copy-done.2
  (35 shorter events, 0.4 us)
Async XLA Ops:
  7.2 4.4 %copy-start = (bf16[1,4096,128]{2,1,0:T(8,128)(2,1)S(1)}, bf16[1,4096,128]{2,1,0:T(8,128)(2,1)}, u32[]{:S(2)}) copy-start(bf16[1,4096,128]{2,1,0:T(8,128)(2,1)} %param.11) | copy-start | bytes 3145732
  7.2 4.4 %copy-start.1 = (bf16[1,128,4096]{2,1,0:T(8,128)(2,1)S(1)}, bf16[1,128,4096]{2,1,0:T(8,128)(2,1)}, u32[]{:S(2)}) copy-start(bf16[1,128,4096]{2,1,0:T(8,128)(2,1)} %param.8) | copy-start | bytes 3145732
  7.2 4.4 %copy-start.3 = (f32[1,4096]{1,0:T(1,128)S(1)}, f32[1,4096]{1,0:T(1,128)}, u32[]{:S(2)}) copy-start(f32[1,4096]{1,0:T(1,128)} %param.12) | copy-start | bytes 49156
  7.2 4.4 %copy-start.4 = (bf16[1,128,128]{2,1,0:T(8,128)(2,1)S(1)}, bf16[1,128,128]{2,1,0:T(8,128)(2,1)}, u32[]{:S(2)}) copy-start(bf16[1,128,128]{2,1,0:T(8,128)(2,1)} %param.10) | copy-start | bytes 98308
  7.2 326.5 %all-reduce.3.cloned.1.call-start = ((), (), s32[]{:S(2)}) async-start(), calls=%async_computation | async-start | bytes 4227072
  335.3 6.9 %collective-permute-start = (bf16[16,4096]{1,0:T(8,128)(2,1)S(1)}, bf16[16,4096]{1,0:T(8,128)(2,1)S(1)}, u32[]{:S(2)}, u32[]{:S(2)}) collective-permute-start(bf16[16,4096]{1,0:T(8,128)(2,1)S(1)} %broadcast_select_fusion.5), channel_id=1, source_target_pairs={{1,0},{2,1},{3,2},{5,4},{6,5},{7,6},{9,8},{10,9},{11,10},{13,12},{... | collective-permute-start | bytes 393224 | tf_op jit(solution)/shard_map/while/body/eval_jaxpr/ppermute | solution.py:14
  343.3 6.9 %collective-permute-start = (bf16[16,4096]{1,0:T(8,128)(2,1)S(1)}, bf16[16,4096]{1,0:T(8,128)(2,1)S(1)}, u32[]{:S(2)}, u32[]{:S(2)}) collective-permute-start(bf16[16,4096]{1,0:T(8,128)(2,1)S(1)} %broadcast_select_fusion.5), channel_id=1, source_target_pairs={{1,0},{2,1},{3,2},{5,4},{6,5},{7,6},{9,8},{10,9},{11,10},{13,12},{... | collective-permute-start | bytes 393224 | tf_op jit(solution)/shard_map/while/body/eval_jaxpr/ppermute | solution.py:14
  351.2 6.9 %collective-permute-start = (bf16[16,4096]{1,0:T(8,128)(2,1)S(1)}, bf16[16,4096]{1,0:T(8,128)(2,1)S(1)}, u32[]{:S(2)}, u32[]{:S(2)}) collective-permute-start(bf16[16,4096]{1,0:T(8,128)(2,1)S(1)} %broadcast_select_fusion.5), channel_id=1, source_target_pairs={{1,0},{2,1},{3,2},{5,4},{6,5},{7,6},{9,8},{10,9},{11,10},{13,12},{... | collective-permute-start | bytes 393224 | tf_op jit(solution)/shard_map/while/body/eval_jaxpr/ppermute | solution.py:14
  359.2 7.3 %collective-permute-start = (bf16[16,4096]{1,0:T(8,128)(2,1)S(1)}, bf16[16,4096]{1,0:T(8,128)(2,1)S(1)}, u32[]{:S(2)}, u32[]{:S(2)}) collective-permute-start(bf16[16,4096]{1,0:T(8,128)(2,1)S(1)} %broadcast_select_fusion.5), channel_id=1, source_target_pairs={{1,0},{2,1},{3,2},{5,4},{6,5},{7,6},{9,8},{10,9},{11,10},{13,12},{... | collective-permute-start | bytes 393224 | tf_op jit(solution)/shard_map/while/body/eval_jaxpr/ppermute | solution.py:14
  367.6 8.1 %collective-permute-start = (bf16[16,4096]{1,0:T(8,128)(2,1)S(1)}, bf16[16,4096]{1,0:T(8,128)(2,1)S(1)}, u32[]{:S(2)}, u32[]{:S(2)}) collective-permute-start(bf16[16,4096]{1,0:T(8,128)(2,1)S(1)} %broadcast_select_fusion.5), channel_id=1, source_target_pairs={{1,0},{2,1},{3,2},{5,4},{6,5},{7,6},{9,8},{10,9},{11,10},{13,12},{... | collective-permute-start | bytes 393224 | tf_op jit(solution)/shard_map/while/body/eval_jaxpr/ppermute | solution.py:14
  376.7 7.2 %collective-permute-start = (bf16[16,4096]{1,0:T(8,128)(2,1)S(1)}, bf16[16,4096]{1,0:T(8,128)(2,1)S(1)}, u32[]{:S(2)}, u32[]{:S(2)}) collective-permute-start(bf16[16,4096]{1,0:T(8,128)(2,1)S(1)} %broadcast_select_fusion.5), channel_id=1, source_target_pairs={{1,0},{2,1},{3,2},{5,4},{6,5},{7,6},{9,8},{10,9},{11,10},{13,12},{... | collective-permute-start | bytes 393224 | tf_op jit(solution)/shard_map/while/body/eval_jaxpr/ppermute | solution.py:14
  385.0 6.9 %collective-permute-start = (bf16[16,4096]{1,0:T(8,128)(2,1)S(1)}, bf16[16,4096]{1,0:T(8,128)(2,1)S(1)}, u32[]{:S(2)}, u32[]{:S(2)}) collective-permute-start(bf16[16,4096]{1,0:T(8,128)(2,1)S(1)} %broadcast_select_fusion.5), channel_id=1, source_target_pairs={{1,0},{2,1},{3,2},{5,4},{6,5},{7,6},{9,8},{10,9},{11,10},{13,12},{... | collective-permute-start | bytes 393224 | tf_op jit(solution)/shard_map/while/body/eval_jaxpr/ppermute | solution.py:14
  393.0 6.9 %collective-permute-start = (bf16[16,4096]{1,0:T(8,128)(2,1)S(1)}, bf16[16,4096]{1,0:T(8,128)(2,1)S(1)}, u32[]{:S(2)}, u32[]{:S(2)}) collective-permute-start(bf16[16,4096]{1,0:T(8,128)(2,1)S(1)} %broadcast_select_fusion.5), channel_id=1, source_target_pairs={{1,0},{2,1},{3,2},{5,4},{6,5},{7,6},{9,8},{10,9},{11,10},{13,12},{... | collective-permute-start | bytes 393224 | tf_op jit(solution)/shard_map/while/body/eval_jaxpr/ppermute | solution.py:14
  400.9 6.9 %collective-permute-start = (bf16[16,4096]{1,0:T(8,128)(2,1)S(1)}, bf16[16,4096]{1,0:T(8,128)(2,1)S(1)}, u32[]{:S(2)}, u32[]{:S(2)}) collective-permute-start(bf16[16,4096]{1,0:T(8,128)(2,1)S(1)} %broadcast_select_fusion.5), channel_id=1, source_target_pairs={{1,0},{2,1},{3,2},{5,4},{6,5},{7,6},{9,8},{10,9},{11,10},{13,12},{... | collective-permute-start | bytes 393224 | tf_op jit(solution)/shard_map/while/body/eval_jaxpr/ppermute | solution.py:14
  408.9 6.9 %collective-permute-start = (bf16[16,4096]{1,0:T(8,128)(2,1)S(1)}, bf16[16,4096]{1,0:T(8,128)(2,1)S(1)}, u32[]{:S(2)}, u32[]{:S(2)}) collective-permute-start(bf16[16,4096]{1,0:T(8,128)(2,1)S(1)} %broadcast_select_fusion.5), channel_id=1, source_target_pairs={{1,0},{2,1},{3,2},{5,4},{6,5},{7,6},{9,8},{10,9},{11,10},{13,12},{... | collective-permute-start | bytes 393224 | tf_op jit(solution)/shard_map/while/body/eval_jaxpr/ppermute | solution.py:14
  416.8 6.9 %collective-permute-start = (bf16[16,4096]{1,0:T(8,128)(2,1)S(1)}, bf16[16,4096]{1,0:T(8,128)(2,1)S(1)}, u32[]{:S(2)}, u32[]{:S(2)}) collective-permute-start(bf16[16,4096]{1,0:T(8,128)(2,1)S(1)} %broadcast_select_fusion.5), channel_id=1, source_target_pairs={{1,0},{2,1},{3,2},{5,4},{6,5},{7,6},{9,8},{10,9},{11,10},{13,12},{... | collective-permute-start | bytes 393224 | tf_op jit(solution)/shard_map/while/body/eval_jaxpr/ppermute | solution.py:14
  424.8 1.0 copy-start.2
Sparse Core Ops, SparseCore 0:
  15.2 318.5 all-reduce.2
where the time goes:
time: 433 us
  waiting for transfers between devices  363 us (84%)
  starting transfers between devices  27.2 us (6%)
  other arithmetic  19 us (4%)
  between operations  14.8 us (3%)
    unnamed x2, waiting for transfers between devices  313 us
    ppermute x11, waiting for transfers between devices, from_behind(): return lax.ppermute(array, axis, pairs)  49.8 us
    ppermute x11, starting transfers between devices, from_behind(): return lax.ppermute(array, axis, pairs)  27.1 us
    dynamic_update_slice x11, other arithmetic, advance(): lax.dynamic_update_index_in_dim(result, jnp.where(usable, updated, curren...  11.5 us
  transfers between devices with their start and end apart: 12, of which 12 were waited for; matrix products, arithmetic and copies ran while one was open for 1% of the time, Pallas kernels for 0%

commit v1 on v0

v1 whole, which is shorter than its diff:
```python
import math

import jax
import jax.numpy as jnp
from jax import lax
from jax.experimental import pallas as pl
from jax.experimental.pallas import tpu as pltpu
from jax.sharding import PartitionSpec as P

EPS = 1e-05
MESH_ID = pl.DeviceIdType.MESH
F32, BF16 = jnp.float32, jnp.bfloat16

ROWS, WIDTH, VAL = 128, 4096, 128
MICRO, SLOTS = 8, 16
NZ, NY = 12, 8
BLOCK = 43
HALF = 24
ZROWS = NY * HALF

C1, C2 = 11 * 128, 22 * 128
STEP = 512


def pieces(low, high):
    return [(a, min(STEP, high - a)) for a in range(low, high, STEP)]


def kernel(
    counts, x_hbm, top_hbm, vg_hbm, w_hbm, g_hbm,
    out, owned,
    x, top, vg, w, g, br, nm, mk, ga, gx, gp, msg, rm, rp,
    pk, pf, zs, zr, ys, yr, rolled,
    lsem, ms, mr, ps, pr, xs, xr, zss, zrs, yss, yrs,
):
    dp = lax.axis_index("dp")
    sec = lax.axis_index("section")
    core = lax.rem(dp, 2)
    yy = lax.rem(lax.div(dp, 2), NY)
    zz = lax.div(dp, 2 * NY)

    def at(z, y, c):
        return (z * NY + y) * 2 + c

    behind = (dp, lax.rem(sec + 3, 4))
    ahead = (dp, lax.rem(sec + 1, 4))
    twin = (at(zz, yy, 1 - core), sec)
    zplus = (at(lax.rem(zz + 1, NZ), yy, core), sec)
    zminus = (at(lax.rem(zz + NZ - 1, NZ), yy, core), sec)
    yplus = (at(zz, lax.rem(yy + 1, NY), core), sec)
    yminus = (at(zz, lax.rem(yy + NY - 1, NY), core), sec)

    loads = [
        pltpu.make_async_copy(s, d, lsem.at[i])
        for i, (s, d) in enumerate(
            [(vg_hbm, vg), (w_hbm, w), (x_hbm, x), (g_hbm, g), (top_hbm, top)]
        )
    ]
    for cp in loads:
        cp.start()
    barrier = pltpu.get_barrier_semaphore()
    for peer in (behind, ahead, twin, zplus, zminus, yplus, yminus):
        pl.semaphore_signal(barrier, inc=1, device_id=peer, device_id_type=MESH_ID)

    def remote(src, dst, ssem, rsem, peer):
        return pltpu.make_async_remote_copy(
            src_ref=src, dst_ref=dst, send_sem=ssem, recv_sem=rsem,
            device_id=peer, device_id_type=MESH_ID,
        )

    def rows(k):
        return pl.ds(pl.multiple_of(k * SLOTS, SLOTS), SLOTS)

    def part(low, high):
        return pl.ds(low, high - low)

    def minus_cd(k, high):
        here = (rows(k), part(0, high))
        return remote(out.at[here], rm.at[here], ms.at[0, k], mr.at[0, k], behind)

    def minus_x(k):
        here = (rows(k), part(C2, WIDTH))
        return remote(msg.at[here], rm.at[here], ms.at[1, k], mr.at[1, k], behind)

    def plus_d(k):
        here = (rows(k), part(C1, C2))
        return remote(msg.at[here], rp.at[here], ps.at[0, k], pr.at[0, k], ahead)

    def plus_x(k, src):
        here = (rows(k), part(C2, WIDTH))
        return remote(src.at[here], rp.at[here], ps.at[1, k], pr.at[1, k], ahead)

    loads[0].wait()
    slot = lax.broadcasted_iota(jnp.int32, (SLOTS, VAL), 0)
    for m in range(MICRO):
        here = pl.ds(m * SLOTS, SLOTS)
        value = vg[here, :].astype(F32)
        mk[here, :] = jnp.where(slot < counts[0, m], value, 0.0).astype(BF16)
    loads[1].wait()
    for a in range(0, WIDTH, 1024):
        br[:, a : a + 1024] = lax.dot_general(
            mk[0:ROWS, :], w[a : a + 1024, :], (((1,), (1,)), ((), ())),
            preferred_element_type=F32,
        )
    loads[2].wait()
    loads[3].wait()
    loads[4].wait()
    ga[...] = jnp.zeros_like(ga)
    pl.semaphore_wait(barrier, 7)

    def first(k, carry):
        r = rows(k)
        square = jnp.zeros((SLOTS, 128), F32)
        cross = jnp.zeros((SLOTS, 128), F32)
        for a, n in pieces(0, WIDTH):
            xa = x[r, a : a + n].astype(F32)
            gb = g[0:1, a : a + n] * br[r, a : a + n]
            s2, c2 = xa * xa, xa * gb
            for j in range(0, n, 128):
                square = square + s2[:, j : j + 128]
                cross = cross + c2[:, j : j + 128]
        scale = lax.rsqrt(jnp.sum(square, axis=1, keepdims=True) * (1.0 / WIDTH) + EPS)
        mean = jnp.sum(cross, axis=1, keepdims=True) * scale * (1.0 / WIDTH)
        for a, n in pieces(0, WIDTH):
            cols = slice(a, a + n)
            unit = x[r, cols].astype(F32) * scale
            gr = g[0:1, cols]
            back = br[r, cols]
            nm[r, cols] = (unit * gr).astype(BF16)
            prod = unit * back
            ga[:, cols] += prod[0:8] + prod[8:16]
            br[r, cols] = scale * (gr * back - unit * mean)

        @pl.when(sec == 3)
        def _():
            for a, n in pieces(0, WIDTH):
                cols = slice(a, a + n)
                out[r, cols] = (top[r, cols].astype(F32) + br[r, cols]).astype(BF16)
            minus_cd(k, C2).start()

        @pl.when(sec == 1)
        def _():
            for a, n in pieces(C1, WIDTH):
                msg[r, a : a + n] = br[r, a : a + n].astype(BF16)
            plus_d(k).start()
            minus_x(k).start()

        @pl.when(sec == 2)
        def _():
            for a, n in pieces(C2, WIDTH):
                msg[r, a : a + n] = br[r, a : a + n].astype(BF16)
            plus_x(k, msg).start()

        return carry

    lax.fori_loop(0, MICRO, first, 0)

    for j in range(WIDTH // 128):
        gx[j : j + 1, :] = jnp.sum(ga[:, j * 128 : j * 128 + 128], axis=0, keepdims=True)
    swaps = [
        remote(nm.at[pl.ds(0, ROWS)], nm.at[pl.ds(ROWS, ROWS)], xs.at[0], xr.at[0], twin),
        remote(mk.at[pl.ds(0, ROWS)], mk.at[pl.ds(ROWS, ROWS)], xs.at[1], xr.at[1], twin),
        remote(gx, gp, xs.at[2], xr.at[2], twin),
    ]
    for cp in swaps:
        cp.start()

    def node3_d(k):
        plus_d(k).wait_recv()
        r = rows(k)
        for a, n in pieces(C1, C2):
            msg[r, a : a + n] = (rp[r, a : a + n].astype(F32) + br[r, a : a + n]).astype(BF16)
        plus_d(k).start()

    def node3_x(k):
        plus_x(k, msg).wait_recv()
        r = rows(k)
        for a, n in pieces(C2, WIDTH):
            msg[r, a : a + n] = (rp[r, a : a + n].astype(F32) + br[r, a : a + n]).astype(BF16)
        plus_x(k, msg).start()

    def node2_cd(k):
        minus_cd(k, C2).wait_recv()
        r = rows(k)
        for a, n in pieces(0, C2):
            out[r, a : a + n] = (rm[r, a : a + n].astype(F32) + br[r, a : a + n]).astype(BF16)
        minus_cd(k, C2).start()

    def node2_x(k):
        plus_x(k, msg).wait_recv()
        r = rows(k)
        for a, n in pieces(C2, WIDTH):
            out[r, a : a + n] = (
                top[r, a : a + n].astype(F32) + rp[r, a : a + n].astype(F32)
            ).astype(BF16)

    def node1_cd(k):
        minus_cd(k, C2).wait_recv()
        r = rows(k)
        for a, n in pieces(0, C1):
            out[r, a : a + n] = (rm[r, a : a + n].astype(F32) + br[r, a : a + n]).astype(BF16)
        minus_cd(k, C1).start()
        for a, n in pieces(C1, C2):
            out[r, a : a + n] = (rm[r, a : a + n].astype(F32) + br[r, a : a + n]).astype(BF16)

    def node1_x(k):
        plus_x(k, rp).wait_recv()
        plus_x(k, rp).start()
        r = rows(k)
        for a, n in pieces(C2, WIDTH):
            total = top[r, a : a + n].astype(F32) + rp[r, a : a + n].astype(F32)
            out[r, a : a + n] = (total + br[r, a : a + n]).astype(BF16)

    def node0_x_forward(k):
        plus_x(k, rp).wait_recv()
        plus_x(k, rp).start()

    def node0_x(k):
        minus_x(k).wait_recv()
        r = rows(k)
        for a, n in pieces(C2, WIDTH):
            total = top[r, a : a + n].astype(F32) + rp[r, a : a + n].astype(F32)
            total = total + rm[r, a : a + n].astype(F32)
            out[r, a : a + n] = (total + br[r, a : a + n]).astype(BF16)

    def node0_d(k):
        plus_d(k).wait_recv()
        r = rows(k)
        for a, n in pieces(C1, C2):
            total = top[r, a : a + n].astype(F32) + rp[r, a : a + n].astype(F32)
            out[r, a : a + n] = (total + br[r, a : a + n]).astype(BF16)

    def node0_c(k):
        minus_cd(k, C1).wait_recv()
        r = rows(k)
        for a, n in pieces(0, C1):
            out[r, a : a + n] = (rm[r, a : a + n].astype(F32) + br[r, a : a + n]).astype(BF16)

    script = [
        (3, node3_x, 0), (3, node3_d, 0),
        (2, node3_d, 0), (2, node2_cd, 0), (2, node2_x, 3),
        (1, node1_cd, 0), (1, node1_x, 1),
        (0, node0_x_forward, 0), (0, node0_x, 1), (0, node0_d, 1), (0, node0_c, 2),
    ]

    def chain(i):
        for section in range(4):
            todo = [
                (step, i - lag) for s, step, lag in script
                if s == section and 0 <= i - lag < MICRO
            ]
            if not todo:
                continue

            @pl.when(sec == section)
            def _(todo=todo):
                for step, k in todo:
                    step(k)

    def z_copy(i, peer):
        return remote(zs.at[i], zr.at[i], zss.at[i], zrs.at[i], peer)

    def z_step(s):
        up = pf[lax.rem(zz + 6 - s, NZ)]
        if s > 0:
            z_copy(s - 1, zplus).wait_recv()
            up = up + zr[s - 1].astype(F32)
        zs[s] = up.astype(BF16)
        z_copy(s, zplus).start()
        if s < 5:
            down = pf[lax.rem(zz + NZ - 5 + s, NZ)]
            if s > 0:
                z_copy(6 + s - 1, zminus).wait_recv()
                down = down + zr[6 + s - 1].astype(F32)
            zs[6 + s] = down.astype(BF16)
            z_copy(6 + s, zminus).start()

    def z_last():
        z_copy(5, zplus).wait_recv()
        z_copy(10, zminus).wait_recv()
        pf[zz] = pf[zz] + zr[5].astype(F32) + zr[10].astype(F32)

    def y_own(y):
        return pf[zz, pl.ds(pl.multiple_of(y * HALF, 8), HALF), :]

    def y_copy(i, peer):
        return remote(ys.at[i], yr.at[i], yss.at[i], yrs.at[i], peer)

    def y_step(s):
        up = y_own(lax.rem(yy + 4 - s, NY))
        if s > 0:
            y_copy(s - 1, yplus).wait_recv()
            up = up + yr[s - 1]
        ys[s] = up
        y_copy(s, yplus).start()
        if s < 3:
            down = y_own(lax.rem(yy + NY - 3 + s, NY))
            if s > 0:
                y_copy(4 + s - 1, yminus).wait_recv()
                down = down + yr[4 + s - 1]
            ys[4 + s] = down
            y_copy(4 + s, yminus).start()

    def y_last():
        y_copy(3, yplus).wait_recv()
        y_copy(6, yminus).wait_recv()
        total = (y_own(yy) + yr[3] + yr[6]) * (1.0 / math.sqrt(ROWS * 2 * NY * NZ))
        rolled[0:HALF, :] = pltpu.roll(total, 64, 1)
        lane = lax.broadcasted_iota(jnp.int32, (HALF, 128), 1)
        late = jnp.where(lane < 64, rolled[0:HALF, :], rolled[1 : HALF + 1, :])
        mine = jnp.where(core == 1, late, total)
        for j in range(21):
            owned[0:1, j * 128 : j * 128 + 128] = mine[j : j + 1, :]
        owned[0:1, 2688:2752] = mine[21:22, 0:64]

    for cp in swaps:
        cp.wait()
    pk[0:32, :] = gx[...] + gp[...]
    for a in range(0, WIDTH, 512):
        pk[32 + a : 32 + a + 512, :] = lax.dot_general(
            nm[:, a : a + 512], mk[...], (((0,), (0,)), ((), ())),
            preferred_element_type=F32,
        )

    def pack(z, carry):
        for y in range(NY):
            start = z * (NY * BLOCK) + y * BLOCK + core * 21
            pf[z, y * HALF : y * HALF + HALF, :] = pk[pl.ds(start, HALF), :]
        return carry

    pk[4128:4136, :] = jnp.zeros((8, 128), F32)
    lax.fori_loop(0, NZ, pack, 0)

    z_step(0)
    chain(0)
    for i in range(1, 6):
        z_step(i)
        chain(i)
    z_last()
    y_step(0)
    chain(6)
    y_step(1)
    chain(7)
    y_step(2)
    chain(8)
    y_step(3)
    chain(9)
    y_last()
    chain(10)

    for i in range(11):
        z_copy(i, zplus).wait_send()
    for i in range(7):
        y_copy(i, yplus).wait_send()

    def drain(k, carry):
        @pl.when(sec >= 2)
        def _():
            minus_cd(k, C2).wait_send()

        @pl.when(sec == 1)
        def _():
            minus_cd(k, C1).wait_send()
            minus_x(k).wait_send()

        @pl.when(sec >= 1)
        def _():
            plus_d(k).wait_send()

        plus_x(k, msg).wait_send()
        return carry

    lax.fori_loop(0, MICRO, drain, 0)


def shards(layer_inputs, top_grad, value_grads, weights, norm_gains, counts):
    anywhere = pl.BlockSpec(memory_space=pl.ANY)
    local = pl.BlockSpec(memory_space=pltpu.VMEM)
    dma = pltpu.SemaphoreType.DMA
    wide = (ROWS, WIDTH)
    grads, owned = pl.pallas_call(
        kernel,
        out_shape=(
            jax.ShapeDtypeStruct(wide, BF16),
            jax.ShapeDtypeStruct((1, 2752), F32),
        ),
        in_specs=[pl.BlockSpec(memory_space=pltpu.SMEM)] + [anywhere] * 5,
        out_specs=(local, local),
        scratch_shapes=[
            pltpu.VMEM(wide, BF16),
            pltpu.VMEM(wide, BF16),
            pltpu.VMEM((ROWS, VAL), BF16),
            pltpu.VMEM((WIDTH, VAL), BF16),
            pltpu.VMEM((1, WIDTH), F32),
            pltpu.VMEM(wide, F32),
            pltpu.VMEM((2 * ROWS, WIDTH), BF16),
            pltpu.VMEM((2 * ROWS, VAL), BF16),
            pltpu.VMEM((8, WIDTH), F32),
            pltpu.VMEM((32, 128), F32),
            pltpu.VMEM((32, 128), F32),
            pltpu.VMEM(wide, BF16),
            pltpu.VMEM(wide, BF16),
            pltpu.VMEM(wide, BF16),
            pltpu.VMEM((4136, 128), F32),
            pltpu.VMEM((NZ, ZROWS, 128), F32),
            pltpu.VMEM((11, ZROWS, 128), BF16),
            pltpu.VMEM((11, ZROWS, 128), BF16),
            pltpu.VMEM((7, HALF, 128), F32),
            pltpu.VMEM((7, HALF, 128), F32),
            pltpu.VMEM((HALF + 8, 128), F32),
            dma((5,)),
            dma((2, MICRO)), dma((2, MICRO)), dma((2, MICRO)), dma((2, MICRO)),
            dma((3,)), dma((3,)),
            dma((11,)), dma((11,)), dma((7,)), dma((7,)),
        ],
        compiler_params=pltpu.CompilerParams(
            collective_id=0, has_side_effects=True, vmem_limit_bytes=40 * 2**20
        ),
    )(
        counts.reshape(1, MICRO), layer_inputs[0], top_grad, value_grads[0],
        weights[0], norm_gains,
    )
    return grads.reshape(1, ROWS, WIDTH), owned


def solution(mesh):
    placed = (
        P("section", "dp", None),
        P("dp", None),
        P("section", "dp", None),
        P("section", None, None),
        P("section", None),
        P("dp"),
    )
    return jax.shard_map(
        shards,
        mesh=mesh,
        in_specs=placed,
        out_specs=(P("section", "dp", None), P("section", "dp")),
        check_vma=False,
    )
```

time: 433 us -> 65.9 us (0.15)
  the two profiles are of different devices: /device:TPU:26 before, /device:TPU:2 now
where the time goes in v1:
time: 65.9 us; the launch traced here: 65.5 us
  Pallas kernels  57.5 us (87%)
  local copies, waits for them, and re-layouts  7.37 us (11%)
    pallas_call x1, Pallas kernels, shards(): pl.pallas_call(kernel, out_shape=(jax.ShapeDtypeStruct(wide, BF16), jax.S...  57.5 us
    unnamed x14, local copies, waits for them, and re-layouts  7.37 us

profile of v1, /device:TPU:2, one launch (start us, length us, event | category | flops | bytes accessed | tf_op | source)
XLA Modules:
  0.0 65.5 jit_solution(11992646220118197844)
XLA Ops:
  0.6 0.0 copy-start.5
  0.6 0.6 copy-done.5
  1.3 0.0 copy-start
  1.3 1.2 %copy-done = bf16[1,128,4096]{2,1,0:T(8,128)(2,1)S(1)} copy-done((bf16[1,128,4096]{2,1,0:T(8,128)(2,1)S(1)}, bf16[1,128,4096]{2,1,0:T(8,128)(2,1)}, u32[]{:S(2)}) %copy-start) | copy-done | bytes 1048600
  2.5 0.0 copy-start.1
  2.5 1.2 %copy-done.1 = bf16[128,4096]{1,0:T(8,128)(2,1)S(1)} copy-done((bf16[128,4096]{1,0:T(8,128)(2,1)S(1)}, bf16[128,4096]{1,0:T(8,128)(2,1)}, u32[]{:S(2)}) %copy-start.1) | copy-done | bytes 1048600
  3.7 0.0 copy-start.2
  3.7 1.2 %copy-done.2 = bf16[1,4096,128]{2,1,0:T(8,128)(2,1)S(1)} copy-done((bf16[1,4096,128]{2,1,0:T(8,128)(2,1)S(1)}, bf16[1,4096,128]{2,1,0:T(8,128)(2,1)}, u32[]{:S(2)}) %copy-start.2) | copy-done | bytes 1048600
  5.0 0.0 copy-start.3
  5.0 0.8 %copy-done.3 = bf16[1,128,128]{2,1,0:T(8,128)(2,1)S(1)} copy-done((bf16[1,128,128]{2,1,0:T(8,128)(2,1)S(1)}, bf16[1,128,128]{2,1,0:T(8,128)(2,1)}, u32[]{:S(2)}) %copy-start.3) | copy-done | bytes 32792
  5.7 0.0 copy-start.4
  5.7 0.7 %copy-done.4 = f32[1,4096]{1,0:T(1,128)S(1)} copy-done((f32[1,4096]{1,0:T(1,128)S(1)}, f32[1,4096]{1,0:T(1,128)}, u32[]{:S(2)}) %copy-start.4) | copy-done | bytes 16408
  6.4 57.5 %shard_map.77 = (bf16[128,4096]{1,0:T(8,128)(2,1)S(1)}, f32[1,2752]{1,0:T(1,128)S(1)}) custom-call(s32[1,8]{1,0:T(1,128)S(1)} %bitcast.9, bf16[128,4096]{1,0:T(8,128)(2,1)S(1)} %bitcast.5, bf16[128,4096]{1,0:T(8,128)(2,1)S(1)} %copy-done.1, bf16[128,128]{1,0:T(8,128)(2,1)S(1)} %bitcast.8, bf16[4096,128]{1,0:T(8,128)(2,1)S(1)} %bitcast.6, f32[1,4096]{1,0:T(1,128)S(1)} %copy-done.4), custom_call_target="tpu_custom_call" | custom-call | tf_op jit(solution)/shard_map/pallas_call | solution.py:381
  63.9 1.0 %copy.10 = bf16[1,128,4096]{2,1,0:T(8,128)(2,1)} copy(bf16[1,128,4096]{2,1,0:T(8,128)(2,1)S(1)} %bitcast.7) | data formatting | bytes 2097152
  64.9 0.6 copy.11
Async XLA Ops:
  0.6 0.7 %copy-start.5 = (s32[8]{0:T(128)S(1)}, s32[8]{0:T(128)}, u32[]{:S(2)}) copy-start(s32[8]{0:T(128)} %param.11) | copy-start | bytes 100
  1.3 1.2 %copy-start = (bf16[1,128,4096]{2,1,0:T(8,128)(2,1)S(1)}, bf16[1,128,4096]{2,1,0:T(8,128)(2,1)}, u32[]{:S(2)}) copy-start(bf16[1,128,4096]{2,1,0:T(8,128)(2,1)} %param.6) | copy-start | bytes 3145732
  2.5 1.2 %copy-start.1 = (bf16[128,4096]{1,0:T(8,128)(2,1)S(1)}, bf16[128,4096]{1,0:T(8,128)(2,1)}, u32[]{:S(2)}) copy-start(bf16[128,4096]{1,0:T(8,128)(2,1)} %top_hbm.1) | copy-start | bytes 3145732
  3.7 1.2 %copy-start.2 = (bf16[1,4096,128]{2,1,0:T(8,128)(2,1)S(1)}, bf16[1,4096,128]{2,1,0:T(8,128)(2,1)}, u32[]{:S(2)}) copy-start(bf16[1,4096,128]{2,1,0:T(8,128)(2,1)} %param.9) | copy-start | bytes 3145732
  5.0 0.8 %copy-start.3 = (bf16[1,128,128]{2,1,0:T(8,128)(2,1)S(1)}, bf16[1,128,128]{2,1,0:T(8,128)(2,1)}, u32[]{:S(2)}) copy-start(bf16[1,128,128]{2,1,0:T(8,128)(2,1)} %param.8) | copy-start | bytes 98308
  5.7 0.7 %copy-start.4 = (f32[1,4096]{1,0:T(1,128)S(1)}, f32[1,4096]{1,0:T(1,128)}, u32[]{:S(2)}) copy-start(f32[1,4096]{1,0:T(1,128)} %g_hbm.1) | copy-start | bytes 49156

commit v2 on v1

v2 whole, which is shorter than its diff:
```python
import math

import jax
import jax.numpy as jnp
from jax import lax
from jax.experimental import pallas as pl
from jax.experimental.pallas import tpu as pltpu
from jax.sharding import PartitionSpec as P

EPS = 1e-05
MESH_ID = pl.DeviceIdType.MESH
F32, BF16 = jnp.float32, jnp.bfloat16

ROWS, WIDTH, VAL = 128, 4096, 128
MICRO, SLOTS = 8, 16
NZ, NY = 12, 8
BLOCK = 43
HALF = 24
PAIR = 2 * HALF
GROUPS = ((0, 2), (2, 6), (6, 12))

C1, C2 = 11 * 128, 22 * 128
STEP = 512

ORDER = (
    (
        (),
        (("b", 0),),
        (("c", 0),),
        (("x", 0),),
    ),
    (
        (("xf", 0), ("x", 0), ("xf", 1), ("x", 1), ("c", 0), ("xf", 2), ("x", 2), ("xf", 3), ("xf", 4), ("c", 1), ("xf", 5), ("x", 3)),
        (("b", 1), ("c", 0), ("b", 2), ("c", 1), ("b", 3), ("x", 0), ("c", 2), ("c", 3), ("b", 4), ("x", 1), ("c", 4), ("x", 2)),
        (("c", 1), ("c", 2), ("d", 0), ("d", 1), ("d", 2), ("c", 3), ("d", 3), ("c", 4), ("d", 4), ("c", 5), ("d", 5), ("c", 6), ("d", 6), ("c", 7), ("d", 7), ("e", 0), ("x", 0), ("e", 1)),
        (("x", 1), ("x", 2), ("x", 3), ("x", 4), ("x", 5), ("x", 6), ("x", 7), ("d", 0), ("d", 1)),
    ),
    (
        (("xf", 6), ("c", 2), ("xf", 7), ("c", 3), ("d", 0), ("x", 4), ("d", 1)),
        (("c", 5), ("b", 5), ("x", 3), ("c", 6), ("x", 4), ("c", 7), ("b", 6), ("x", 5), ("e", 0), ("x", 6)),
        (("e", 2), ("x", 1), ("e", 3), ("x", 2), ("e", 4), ("x", 3)),
        (("d", 2), ("d", 3), ("d", 4), ("d", 5)),
    ),
    (
        (("c", 4), ("d", 2), ("c", 5), ("d", 3), ("x", 5), ("d", 4), ("c", 6), ("d", 5), ("c", 7), ("d", 6), ("x", 6)),
        (("e", 1), ("x", 7), ("b", 7), ("e", 2), ("e", 3), ("e", 4), ("e", 5), ("e", 6)),
        (("e", 5), ("x", 4), ("e", 6), ("x", 5), ("e", 7), ("x", 6), ("x", 7)),
        (("d", 6), ("d", 7)),
    ),
    (
        (("d", 7), ("x", 7)),
        (("e", 7),),
        (),
        (),
    ),
)


def pieces(low, high):
    return [(a, min(STEP, high - a)) for a in range(low, high, STEP)]


def kernel(
    counts, x_hbm, top_hbm, vg_hbm, w_hbm, g_hbm,
    out, owned,
    x, top, vg, w, g, br, nm, mk, ga, gx, gp, msg, rm, rp,
    pk, zs, zr, ys, yr, half, rolled,
    lsem, ms, mr, ps, pr, xs, xr, zss, zrs, yss, yrs, hs, hr, hello,
):
    dp = lax.axis_index("dp")
    sec = lax.axis_index("section")
    core = lax.rem(dp, 2)
    yy = lax.rem(lax.div(dp, 2), NY)
    zz = lax.div(dp, 2 * NY)

    def at(z, y, c):
        return (z * NY + y) * 2 + c

    behind = (dp, lax.rem(sec + 3, 4))
    ahead = (dp, lax.rem(sec + 1, 4))
    twin = (at(zz, yy, 1 - core), sec)
    lead = core == 0

    def on_y(d):
        return (at(zz, lax.rem(yy + d, NY), 0), sec)

    def on_z(d):
        return (at(lax.rem(zz + d, NZ), yy, 0), sec)

    loads = [
        pltpu.make_async_copy(s, d, lsem.at[i])
        for i, (s, d) in enumerate(
            [(vg_hbm, vg), (w_hbm, w), (x_hbm, x), (g_hbm, g), (top_hbm, top)]
        )
    ]
    for cp in loads:
        cp.start()
    barrier = pltpu.get_barrier_semaphore()
    def signal(sem, peer):
        pl.semaphore_signal(sem, inc=1, device_id=peer, device_id_type=MESH_ID)

    signal(barrier, behind)
    signal(barrier, ahead)

    @pl.when(lead)
    def _():
        signal(barrier, twin)
        for d in range(1, NY):
            pl.when(yy + d < NY)(lambda d=d: signal(barrier, on_y(d)))
        for d in range(1, NZ):
            pl.when(zz + d < NZ)(lambda d=d: signal(barrier, on_z(d)))

    def remote(src, dst, ssem, rsem, peer):
        return pltpu.make_async_remote_copy(
            src_ref=src, dst_ref=dst, send_sem=ssem, recv_sem=rsem,
            device_id=peer, device_id_type=MESH_ID,
        )

    def rows(k):
        return pl.ds(pl.multiple_of(k * SLOTS, SLOTS), SLOTS)

    def part(low, high):
        return pl.ds(low, high - low)

    def minus_c(k):
        here = (rows(k), part(0, C1))
        return remote(out.at[here], rm.at[here], ms.at[0, k], mr.at[0, k], behind)

    def minus_d(k):
        here = (rows(k), part(C1, C2))
        return remote(out.at[here], rm.at[here], ms.at[2, k], mr.at[2, k], behind)

    def minus_x(k):
        here = (rows(k), part(C2, WIDTH))
        return remote(msg.at[here], rm.at[here], ms.at[1, k], mr.at[1, k], behind)

    def plus_d(k):
        here = (rows(k), part(C1, C2))
        return remote(msg.at[here], rp.at[here], ps.at[0, k], pr.at[0, k], ahead)

    def plus_x(k, src):
        here = (rows(k), part(C2, WIDTH))
        return remote(src.at[here], rp.at[here], ps.at[1, k], pr.at[1, k], ahead)

    loads[0].wait()
    slot = lax.broadcasted_iota(jnp.int32, (SLOTS, VAL), 0)
    for m in range(MICRO):
        here = pl.ds(m * SLOTS, SLOTS)
        value = vg[here, :].astype(F32)
        mk[here, :] = jnp.where(slot < counts[0, m], value, 0.0).astype(BF16)
    loads[1].wait()
    for a in range(0, WIDTH, 1024):
        br[:, a : a + 1024] = lax.dot_general(
            mk[0:ROWS, :], w[a : a + 1024, :], (((1,), (1,)), ((), ())),
            preferred_element_type=F32,
        )
    loads[2].wait()
    loads[3].wait()
    loads[4].wait()
    ga[...] = jnp.zeros_like(ga)
    pl.semaphore_wait(barrier, jnp.where(lead, 2 + yy + zz, 3))

    @pl.when(lead)
    def _():
        for d in range(1, NY):
            pl.when(yy + d >= NY)(lambda d=d: signal(hello.at[0], on_y(d)))
        for d in range(1, NZ):
            pl.when(zz + d >= NZ)(lambda d=d: signal(hello.at[1], on_z(d)))

    def swap_rows(k):
        there = pl.ds(pl.multiple_of(ROWS + k * SLOTS, SLOTS), SLOTS)
        return remote(nm.at[rows(k)], nm.at[there], xs.at[k], xr.at[k], twin)


    def first(k, carry):
        r = rows(k)
        square = jnp.zeros((SLOTS, 128), F32)
        cross = jnp.zeros((SLOTS, 128), F32)
        for a, n in pieces(0, WIDTH):
            xa = x[r, a : a + n].astype(F32)
            gb = g[0:1, a : a + n] * br[r, a : a + n]
            s2, c2 = xa * xa, xa * gb
            for j in range(0, n, 128):
                square = square + s2[:, j : j + 128]
                cross = cross + c2[:, j : j + 128]
        scale = lax.rsqrt(jnp.sum(square, axis=1, keepdims=True) * (1.0 / WIDTH) + EPS)
        mean = jnp.sum(cross, axis=1, keepdims=True) * scale * (1.0 / WIDTH)
        for a, n in pieces(0, WIDTH):
            cols = slice(a, a + n)
            unit = x[r, cols].astype(F32) * scale
            gr = g[0:1, cols]
            back = br[r, cols]
            nm[r, cols] = (unit * gr).astype(BF16)
            prod = unit * back
            ga[:, cols] += prod[0:8] + prod[8:16]
            br[r, cols] = scale * (gr * back - unit * mean)

        pl.when(core == 1)(lambda: swap_rows(k).start())

        @pl.when(sec == 3)
        def _():
            for a, n in pieces(0, WIDTH):
                cols = slice(a, a + n)
                out[r, cols] = (top[r, cols].astype(F32) + br[r, cols]).astype(BF16)
            minus_c(k).start()

        @pl.when(sec == 1)
        def _():
            for a, n in pieces(C1, WIDTH):
                msg[r, a : a + n] = br[r, a : a + n].astype(BF16)
            plus_d(k).start()

        @pl.when(sec == 2)
        def _():
            for a, n in pieces(C2, WIDTH):
                msg[r, a : a + n] = br[r, a : a + n].astype(BF16)
            plus_x(k, msg).start()

        return carry

    lax.fori_loop(0, MICRO, first, 0)

    @pl.when(sec == 3)
    def _():
        for k in range(MICRO):
            minus_d(k).start()

    for j in range(WIDTH // 128):
        gx[j : j + 1, :] = jnp.sum(ga[:, j * 128 : j * 128 + 128], axis=0, keepdims=True)
    swaps = [
        remote(mk.at[pl.ds(0, ROWS)], mk.at[pl.ds(ROWS, ROWS)], xs.at[8], xr.at[8], twin),
        remote(gx, gp, xs.at[9], xr.at[9], twin),
    ]

    @pl.when(core == 1)
    def _():
        for cp in swaps:
            cp.start()

    def node3_d(k):
        plus_d(k).wait_recv()
        r = rows(k)
        for a, n in pieces(C1, C2):
            msg[r, a : a + n] = (rp[r, a : a + n].astype(F32) + br[r, a : a + n]).astype(BF16)
        plus_d(k).start()

    def node3_x(k):
        plus_x(k, msg).wait_recv()
        r = rows(k)
        for a, n in pieces(C2, WIDTH):
            msg[r, a : a + n] = (rp[r, a : a + n].astype(F32) + br[r, a : a + n]).astype(BF16)
        plus_x(k, msg).start()

    def add_minus(k, low, high):
        r = rows(k)
        for a, n in pieces(low, high):
            out[r, a : a + n] = (rm[r, a : a + n].astype(F32) + br[r, a : a + n]).astype(BF16)

    def relay_c(k):
        minus_c(k).wait_recv()
        add_minus(k, 0, C1)
        minus_c(k).start()

    def node2_e(k):
        minus_d(k).wait_recv()
        add_minus(k, C1, C2)
        minus_d(k).start()

    def node2_x(k):
        plus_x(k, msg).wait_recv()
        r = rows(k)
        for a, n in pieces(C2, WIDTH):
            out[r, a : a + n] = (
                top[r, a : a + n].astype(F32) + rp[r, a : a + n].astype(F32)
            ).astype(BF16)

    def node1_e(k):
        minus_d(k).wait_recv()
        add_minus(k, C1, C2)

    def node1_b(k):
        minus_x(k).start()

    def node1_x(k):
        plus_x(k, rp).wait_recv()
        plus_x(k, rp).start()
        r = rows(k)
        for a, n in pieces(C2, WIDTH):
            total = top[r, a : a + n].astype(F32) + rp[r, a : a + n].astype(F32)
            out[r, a : a + n] = (total + br[r, a : a + n]).astype(BF16)

    def node0_x_forward(k):
        plus_x(k, rp).wait_recv()
        plus_x(k, rp).start()

    def node0_x(k):
        minus_x(k).wait_recv()
        r = rows(k)
        for a, n in pieces(C2, WIDTH):
            total = top[r, a : a + n].astype(F32) + rp[r, a : a + n].astype(F32)
            total = total + rm[r, a : a + n].astype(F32)
            out[r, a : a + n] = (total + br[r, a : a + n]).astype(BF16)

    def node0_d(k):
        plus_d(k).wait_recv()
        r = rows(k)
        for a, n in pieces(C1, C2):
            total = top[r, a : a + n].astype(F32) + rp[r, a : a + n].astype(F32)
            out[r, a : a + n] = (total + br[r, a : a + n]).astype(BF16)

    def node0_c(k):
        minus_c(k).wait_recv()
        add_minus(k, 0, C1)

    steps = (
        {"xf": node0_x_forward, "x": node0_x, "d": node0_d, "c": node0_c},
        {"b": node1_b, "c": relay_c, "e": node1_e, "x": node1_x},
        {"c": relay_c, "d": node3_d, "e": node2_e, "x": node2_x},
        {"x": node3_x, "d": node3_d},
    )

    def chain(stretch):
        for section in range(4):
            todo = ORDER[stretch][section]
            if not todo:
                continue

            @pl.when(sec == section)
            def _(section=section, todo=todo):
                for name, k in todo:
                    steps[section][name](k)

    def owner_rows(z, y):
        start = z * (NY * BLOCK) + y * BLOCK
        return jnp.concatenate([pk[pl.ds(start, HALF), :], pk[pl.ds(start + 21, HALF), :]], axis=0)

    def group_rows(group):
        return pl.ds(group[0] * PAIR, (group[1] - group[0]) * PAIR)

    def y_copy(d, i):
        there = group_rows(GROUPS[i])
        return remote(
            ys.at[lax.rem(yy + d, NY), there], yr.at[NY - d, there],
            yss.at[d, i], yrs.at[NY - d, i], on_y(d),
        )

    def z_copy(z):
        return remote(zs.at[z], zr.at[zz], zss.at[z], zrs.at[zz], (at(z, yy, 0), sec))

    def product():
        for k in range(MICRO):
            swap_rows(k).wait_recv()
        for cp in swaps:
            cp.wait_recv()
        pk[0:32, :] = gx[...] + gp[...]
        for a in range(0, WIDTH, 512):
            pk[32 + a : 32 + a + 512, :] = lax.dot_general(
                nm[:, a : a + 512], mk[...], (((0,), (0,)), ((), ())),
                preferred_element_type=F32,
            )
        pk[4128:4136, :] = jnp.zeros((8, 128), F32)
        pl.when(yy < NY - 1)(lambda: pl.semaphore_wait(hello.at[0], NY - 1 - yy))
        for i, group in enumerate(GROUPS):
            def pack(z, carry):
                for y in range(NY):
                    here = pl.ds(pl.multiple_of(z * PAIR, PAIR), PAIR)
                    ys[y, here, :] = owner_rows(z, y).astype(BF16)
                return carry

            lax.fori_loop(group[0], group[1], pack, 0)
            for d in (4, 3, 5, 2, 6, 1, 7):
                y_copy(d, i).start()

    def y_sum(i):
        low, high = GROUPS[i]
        for d in range(1, NY):
            y_copy(NY - d, i).wait_recv()

        def add(z, carry):
            here = pl.ds(pl.multiple_of(z * PAIR, PAIR), PAIR)
            total = owner_rows(z, yy)
            for d in range(1, NY):
                total = total + yr[d, here, :].astype(F32)
            half[z] = total
            zs[z] = total.astype(BF16)
            return carry

        lax.fori_loop(low, high, add, 0)
        if i == 0:
            zr[zz] = jnp.zeros((PAIR, 128), BF16)
            pl.when(zz < NZ - 1)(lambda: pl.semaphore_wait(hello.at[1], NZ - 1 - zz))
        for z in range(low, high):
            pl.when(zz != z)(lambda z=z: z_copy(z).start())

    def z_arrival(z):
        return remote(zs.at[z], zr.at[z], zss.at[z], zrs.at[z], (at(z, yy, 0), sec))

    give = remote(rolled.at[1], rolled.at[2], hs, hr, twin)
    factor = 1.0 / math.sqrt(ROWS * 2 * NY * NZ)

    def z_sum():
        for z in range(NZ):
            pl.when(zz != z)(lambda z=z: z_arrival(z).wait_recv())
        total = half[zz]
        for z in range(NZ):
            total = total + zr[z].astype(F32)
        total = total * factor
        rolled[1] = total[HALF:PAIR]
        give.start()
        for j in range(21):
            owned[0:1, j * 128 : j * 128 + 128] = total[j : j + 1, :]
        owned[0:1, 2688:2752] = total[21:22, 0:64]

    def twin_last():
        give.wait_recv()
        turned = pltpu.roll(rolled[2], 64, 1)
        rolled[0] = turned
        lane = lax.broadcasted_iota(jnp.int32, (22, 128), 1)
        mine = jnp.where(lane < 64, rolled[0, 0:22, :], rolled[0, 1:23, :])
        for j in range(21):
            owned[0:1, j * 128 : j * 128 + 128] = mine[j : j + 1, :]
        owned[0:1, 2688:2752] = mine[21:22, 0:64]

    chain(0)
    pl.when(lead)(product)
    chain(1)
    pl.when(lead)(lambda: y_sum(0))
    chain(2)
    pl.when(lead)(lambda: y_sum(1))
    chain(3)
    pl.when(lead)(lambda: y_sum(2))
    chain(4)
    pl.when(lead)(z_sum)
    pl.when(core == 1)(twin_last)

    @pl.when(lead)
    def _():
        for i in range(len(GROUPS)):
            for d in range(1, NY):
                y_copy(d, i).wait_send()
        for z in range(NZ):
            pl.when(zz != z)(lambda z=z: z_copy(z).wait_send())
        give.wait_send()

    @pl.when(core == 1)
    def _():
        for k in range(MICRO):
            swap_rows(k).wait_send()
        for cp in swaps:
            cp.wait_send()

    def drain(k, carry):
        @pl.when(sec >= 2)
        def _():
            minus_d(k).wait_send()

        @pl.when(sec == 1)
        def _():
            minus_x(k).wait_send()

        @pl.when(sec >= 1)
        def _():
            minus_c(k).wait_send()
            plus_d(k).wait_send()

        plus_x(k, msg).wait_send()
        return carry

    lax.fori_loop(0, MICRO, drain, 0)


def shards(layer_inputs, top_grad, value_grads, weights, norm_gains, counts):
    anywhere = pl.BlockSpec(memory_space=pltpu.HBM)
    local = pl.BlockSpec(memory_space=pltpu.VMEM)
    dma = pltpu.SemaphoreType.DMA
    wide = (ROWS, WIDTH)
    grads, owned = pl.pallas_call(
        kernel,
        out_shape=(
            jax.ShapeDtypeStruct(wide, BF16),
            jax.ShapeDtypeStruct((1, 2752), F32),
        ),
        in_specs=[pl.BlockSpec(memory_space=pltpu.SMEM)] + [anywhere] * 5,
        out_specs=(local, local),
        scratch_shapes=[
            pltpu.VMEM(wide, BF16),
            pltpu.VMEM(wide, BF16),
            pltpu.VMEM((ROWS, VAL), BF16),
            pltpu.VMEM((WIDTH, VAL), BF16),
            pltpu.VMEM((1, WIDTH), F32),
            pltpu.VMEM(wide, F32),
            pltpu.VMEM((2 * ROWS, WIDTH), BF16),
            pltpu.VMEM((2 * ROWS, VAL), BF16),
            pltpu.VMEM((8, WIDTH), F32),
            pltpu.VMEM((32, 128), F32),
            pltpu.VMEM((32, 128), F32),
            pltpu.VMEM(wide, BF16),
            pltpu.VMEM(wide, BF16),
            pltpu.VMEM(wide, BF16),
            pltpu.VMEM((4136, 128), F32),
            pltpu.VMEM((NZ, PAIR, 128), BF16),
            pltpu.VMEM((NZ, PAIR, 128), BF16),
            pltpu.VMEM((NY, NZ * PAIR, 128), BF16),
            pltpu.VMEM((NY, NZ * PAIR, 128), BF16),
            pltpu.VMEM((NZ, PAIR, 128), F32),
            pltpu.VMEM((3, HALF, 128), F32),
            dma((5,)),
            dma((3, MICRO)), dma((3, MICRO)), dma((2, MICRO)), dma((2, MICRO)),
            dma((10,)), dma((10,)),
            dma((NZ,)), dma((NZ,)),
            dma((NY, len(GROUPS))), dma((NY, len(GROUPS))),
            dma, dma,
            pltpu.SemaphoreType.REGULAR((2,)),
        ],
        compiler_params=pltpu.CompilerParams(
            collective_id=0, has_side_effects=True, vmem_limit_bytes=62 * 2**20
        ),
    )(
        counts.reshape(1, MICRO), layer_inputs[0], top_grad, value_grads[0],
        weights[0], norm_gains,
    )
    return grads.reshape(1, ROWS, WIDTH), owned


def solution(mesh):
    placed = (
        P("section", "dp", None),
        P("dp", None),
        P("section", "dp", None),
        P("section", None, None),
        P("section", None),
        P("dp"),
    )
    return jax.shard_map(
        shards,
        mesh=mesh,
        in_specs=placed,
        out_specs=(P("section", "dp", None), P("section", "dp")),
        check_vma=False,
    )
```

time: 65.9 us -> 43.1 us (0.65)
  the two profiles are of different devices: /device:TPU:2 before, /device:TPU:1 now
where the time goes in v2:
time: 43.1 us; the launch traced here: 42.4 us
  Pallas kernels  38.8 us (90%)
  local copies, waits for them, and re-layouts  2.9 us (7%)
  between operations  0.65 us (2%)
    pallas_call x1, Pallas kernels, shards(): pl.pallas_call(kernel, out_shape=(jax.ShapeDtypeStruct(wide, BF16), jax.S...  38.8 us
    unnamed x4, local copies, waits for them, and re-layouts  2.9 us

profile of v2, /device:TPU:1, one launch (start us, length us, event | category | flops | bytes accessed | tf_op | source)
XLA Modules:
  0.0 42.4 jit_solution(8821350654486091557)
XLA Ops:
  0.6 38.8 %shard_map.77 = (bf16[128,4096]{1,0:T(8,128)(2,1)}, f32[1,2752]{1,0:T(1,128)}) custom-call(s32[1,8]{1,0:T(1,128)} %bitcast.9, bf16[128,4096]{1,0:T(8,128)(2,1)} %bitcast.5, bf16[128,4096]{1,0:T(8,128)(2,1)} %top_hbm.1, bf16[128,128]{1,0:T(8,128)(2,1)} %bitcast.8, bf16[4096,128]{1,0:T(8,128)(2,1)} %bitcast.6, f32[1,4096]{1,0:T(1,128)} %g_hbm.1), custom_call_target="tpu_custom_call" | custom-call | tf_op jit(solution)/shard_map/pallas_call | solution.py:477
  39.5 0.0 copy-start
  39.5 2.3 %copy.10 = bf16[1,128,4096]{2,1,0:T(8,128)(2,1)} copy(bf16[1,128,4096]{2,1,0:T(8,128)(2,1)} %bitcast.7) | data formatting | bytes 2097152
  41.8 0.0 copy-done
  41.8 0.6 %copy.11 = f32[1,2752]{1,0:T(1,128)} copy(f32[1,2752]{1,0:T(1,128)S(1)} %copy-done) | data formatting | bytes 22016
Async XLA Ops:
  39.5 2.3 %copy-start = (f32[1,2752]{1,0:T(1,128)S(1)}, f32[1,2752]{1,0:T(1,128)}, u32[]{:S(2)}) copy-start(f32[1,2752]{1,0:T(1,128)} %get-tuple-element.9) | copy-start | bytes 33028

commit v3 on v2

--- a/solution.py
+++ b/solution.py
@@ -17,7 +17,7 @@
 BLOCK = 43
 HALF = 24
 PAIR = 2 * HALF
-GROUPS = ((0, 2), (2, 6), (6, 12))
+GROUPS = ((0, 2), (2, 5), (5, 8), (8, 12))
 
 C1, C2 = 11 * 128, 22 * 128
 STEP = 512
@@ -26,31 +26,37 @@
     (
         (),
         (("b", 0),),
-        (("c", 0),),
-        (("x", 0),),
+        (),
+        (),
     ),
     (
-        (("xf", 0), ("x", 0), ("xf", 1), ("x", 1), ("c", 0), ("xf", 2), ("x", 2), ("xf", 3), ("xf", 4), ("c", 1), ("xf", 5), ("x", 3)),
-        (("b", 1), ("c", 0), ("b", 2), ("c", 1), ("b", 3), ("x", 0), ("c", 2), ("c", 3), ("b", 4), ("x", 1), ("c", 4), ("x", 2)),
-        (("c", 1), ("c", 2), ("d", 0), ("d", 1), ("d", 2), ("c", 3), ("d", 3), ("c", 4), ("d", 4), ("c", 5), ("d", 5), ("c", 6), ("d", 6), ("c", 7), ("d", 7), ("e", 0), ("x", 0), ("e", 1)),
-        (("x", 1), ("x", 2), ("x", 3), ("x", 4), ("x", 5), ("x", 6), ("x", 7), ("d", 0), ("d", 1)),
+        (("xf", 0),),
+        (("b", 1), ("b", 2), ("c", 0), ("b", 3), ("c", 1), ("c", 2)),
+        (("c", 0), ("d", 0), ("c", 1), ("d", 1), ("c", 2), ("d", 2), ("c", 3), ("d", 3), ("c", 4), ("d", 4), ("c", 5), ("d", 5)),
+        (("x", 0), ("x", 1), ("x", 2), ("x", 3), ("x", 4), ("x", 5), ("x", 6), ("x", 7)),
     ),
     (
-        (("xf", 6), ("c", 2), ("xf", 7), ("c", 3), ("d", 0), ("x", 4), ("d", 1)),
-        (("c", 5), ("b", 5), ("x", 3), ("c", 6), ("x", 4), ("c", 7), ("b", 6), ("x", 5), ("e", 0), ("x", 6)),
-        (("e", 2), ("x", 1), ("e", 3), ("x", 2), ("e", 4), ("x", 3)),
-        (("d", 2), ("d", 3), ("d", 4), ("d", 5)),
+        (("xf", 1), ("xf", 2), ("xf", 3), ("xf", 4), ("xf", 5)),
+        (("b", 4), ("c", 3), ("x", 0), ("c", 4)),
+        (("c", 6), ("d", 6), ("c", 7), ("d", 7), ("e", 0)),
+        (("d", 0), ("d", 1)),
     ),
     (
-        (("c", 4), ("d", 2), ("c", 5), ("d", 3), ("x", 5), ("d", 4), ("c", 6), ("d", 5), ("c", 7), ("d", 6), ("x", 6)),
-        (("e", 1), ("x", 7), ("b", 7), ("e", 2), ("e", 3), ("e", 4), ("e", 5), ("e", 6)),
-        (("e", 5), ("x", 4), ("e", 6), ("x", 5), ("e", 7), ("x", 6), ("x", 7)),
-        (("d", 6), ("d", 7)),
+        (("xf", 6), ("xf", 7)),
+        (("b", 5), ("c", 5), ("x", 1), ("c", 6), ("x", 2), ("b", 6), ("c", 7)),
+        (("e", 1), ("e", 2), ("e", 3)),
+        (("d", 2), ("d", 3)),
     ),
     (
-        (("d", 7), ("x", 7)),
-        (("e", 7),),
         (),
+        (("x", 3), ("x", 4), ("b", 7), ("x", 5)),
+        (("e", 4), ("e", 5), ("e", 6)),
+        (("d", 4), ("d", 5), ("d", 6), ("d", 7)),
+    ),
+    (
+        (("c", 0), ("c", 1), ("c", 2), ("c", 3), ("c", 4), ("c", 5), ("d", 0), ("d", 1), ("c", 6), ("d", 2), ("d", 3), ("d", 4), ("d", 5), ("d", 6), ("x", 0), ("x", 1), ("x", 2), ("c", 7), ("d", 7), ("x", 3), ("x", 4), ("x", 5), ("x", 6), ("x", 7)),
+        (("x", 6), ("e", 0), ("e", 1), ("x", 7), ("e", 2), ("e", 3), ("e", 4), ("e", 5), ("e", 6), ("e", 7)),
+        (("x", 0), ("e", 7), ("x", 1), ("x", 2), ("x", 3), ("x", 4), ("x", 5), ("x", 6), ("x", 7)),
         (),
     ),
 )
@@ -64,7 +70,7 @@
     counts, x_hbm, top_hbm, vg_hbm, w_hbm, g_hbm,
     out, owned,
     x, top, vg, w, g, br, nm, mk, ga, gx, gp, msg, rm, rp,
-    pk, zs, zr, ys, yr, half, rolled,
+    pk, zs, zr, ys, yr, half, rolled, scales, means,
     lsem, ms, mr, ps, pr, xs, xr, zss, zrs, yss, yrs, hs, hr, hello,
 ):
     dp = lax.axis_index("dp")
@@ -185,17 +191,38 @@
                 cross = cross + c2[:, j : j + 128]
         scale = lax.rsqrt(jnp.sum(square, axis=1, keepdims=True) * (1.0 / WIDTH) + EPS)
         mean = jnp.sum(cross, axis=1, keepdims=True) * scale * (1.0 / WIDTH)
+        scales[r, :] = jnp.broadcast_to(scale, (SLOTS, 128))
+        means[r, :] = jnp.broadcast_to(mean, (SLOTS, 128))
         for a, n in pieces(0, WIDTH):
             cols = slice(a, a + n)
             unit = x[r, cols].astype(F32) * scale
-            gr = g[0:1, cols]
-            back = br[r, cols]
-            nm[r, cols] = (unit * gr).astype(BF16)
-            prod = unit * back
+            nm[r, cols] = (unit * g[0:1, cols]).astype(BF16)
+            prod = unit * br[r, cols]
             ga[:, cols] += prod[0:8] + prod[8:16]
-            br[r, cols] = scale * (gr * back - unit * mean)
-
         pl.when(core == 1)(lambda: swap_rows(k).start())
+        return carry
+
+    lax.fori_loop(0, MICRO, first, 0)
+
+    for j in range(WIDTH // 128):
+        gx[j : j + 1, :] = jnp.sum(ga[:, j * 128 : j * 128 + 128], axis=0, keepdims=True)
+    swaps = [
+        remote(mk.at[pl.ds(0, ROWS)], mk.at[pl.ds(ROWS, ROWS)], xs.at[8], xr.at[8], twin),
+        remote(gx, gp, xs.at[9], xr.at[9], twin),
+    ]
+
+    @pl.when(core == 1)
+    def _():
+        for cp in swaps:
+            cp.start()
+
+    def second(k, carry):
+        r = rows(k)
+        scale, mean = scales[r, 0:1], means[r, 0:1]
+        for a, n in pieces(0, WIDTH):
+            cols = slice(a, a + n)
+            unit = x[r, cols].astype(F32) * scale
+            br[r, cols] = scale * (g[0:1, cols] * br[r, cols] - unit * mean)
 
         @pl.when(sec == 3)
         def _():
@@ -218,24 +245,12 @@
 
         return carry
 
-    lax.fori_loop(0, MICRO, first, 0)
+    lax.fori_loop(0, MICRO, second, 0)
 
     @pl.when(sec == 3)
     def _():
         for k in range(MICRO):
             minus_d(k).start()
-
-    for j in range(WIDTH // 128):
-        gx[j : j + 1, :] = jnp.sum(ga[:, j * 128 : j * 128 + 128], axis=0, keepdims=True)
-    swaps = [
-        remote(mk.at[pl.ds(0, ROWS)], mk.at[pl.ds(ROWS, ROWS)], xs.at[8], xr.at[8], twin),
-        remote(gx, gp, xs.at[9], xr.at[9], twin),
-    ]
-
-    @pl.when(core == 1)
-    def _():
-        for cp in swaps:
-            cp.start()
 
     def node3_d(k):
         plus_d(k).wait_recv()
@@ -401,12 +416,14 @@
     def z_sum():
         for z in range(NZ):
             pl.when(zz != z)(lambda z=z: z_arrival(z).wait_recv())
-        total = half[zz]
+        late, total = half[zz, HALF:PAIR], half[zz, 0:HALF]
         for z in range(NZ):
-            total = total + zr[z].astype(F32)
+            late = late + zr[z, HALF:PAIR].astype(F32)
+        rolled[1] = late * factor
+        give.start()
+        for z in range(NZ):
+            total = total + zr[z, 0:HALF].astype(F32)
         total = total * factor
-        rolled[1] = total[HALF:PAIR]
-        give.start()
         for j in range(21):
             owned[0:1, j * 128 : j * 128 + 128] = total[j : j + 1, :]
         owned[0:1, 2688:2752] = total[21:22, 0:64]
@@ -423,13 +440,10 @@
 
     chain(0)
     pl.when(lead)(product)
-    chain(1)
-    pl.when(lead)(lambda: y_sum(0))
-    chain(2)
-    pl.when(lead)(lambda: y_sum(1))
-    chain(3)
-    pl.when(lead)(lambda: y_sum(2))
-    chain(4)
+    for i in range(len(GROUPS)):
+        chain(i + 1)
+        pl.when(lead)(lambda i=i: y_sum(i))
+    chain(len(GROUPS) + 1)
     pl.when(lead)(z_sum)
     pl.when(core == 1)(twin_last)
 
@@ -504,6 +518,8 @@
             pltpu.VMEM((NY, NZ * PAIR, 128), BF16),
             pltpu.VMEM((NZ, PAIR, 128), F32),
             pltpu.VMEM((3, HALF, 128), F32),
+            pltpu.VMEM((ROWS, 128), F32),
+            pltpu.VMEM((ROWS, 128), F32),
             dma((5,)),
             dma((3, MICRO)), dma((3, MICRO)), dma((2, MICRO)), dma((2, MICRO)),
             dma((10,)), dma((10,)),
@@ -513,11 +529,16 @@
             pltpu.SemaphoreType.REGULAR((2,)),
         ],
         compiler_params=pltpu.CompilerParams(
-            collective_id=0, has_side_effects=True, vmem_limit_bytes=62 * 2**20
+            collective_id=0, has_side_effects=True, vmem_limit_bytes=40 * 2**20
         ),
     )(
-        counts.reshape(1, MICRO), layer_inputs[0], top_grad, value_grads[0],
-        weights[0], norm_gains,
+        *(
+            pltpu.with_memory_space_constraint(v, pltpu.HBM)
+            for v in (
+                counts.reshape(1, MICRO), layer_inputs[0], top_grad, value_grads[0],
+                weights[0], norm_gains,
+            )
+        )
     )
     return grads.reshape(1, ROWS, WIDTH), owned
 

time: 43.1 us -> 38.7 us (0.90); the launches traced: 42.4 us -> 38.5 us
  Pallas kernels: 38.8 us -> 36.3 us
  local copies, waits for them, and re-layouts: 2.9 us -> 1.57 us
    pallas_call x1, Pallas kernels: 38.8 us -> 36.3 us  [shards(): pl.pallas_call(kernel, out_shape=(jax.ShapeDtypeStruct(wide, BF16), jax.S...]
    unnamed x4 -> x2, local copies, waits for them, and re-layouts: 2.9 us -> 1.57 us
where the time goes in v3:
time: 38.7 us; the launch traced here: 38.5 us
  Pallas kernels  36.3 us (94%)
  local copies, waits for them, and re-layouts  1.57 us (4%)
  between operations  0.64 us (2%)
    pallas_call x1, Pallas kernels, shards(): pl.pallas_call(kernel, out_shape=(jax.ShapeDtypeStruct(wide, BF16), jax.S...  36.3 us
    unnamed x2, local copies, waits for them, and re-layouts  1.57 us

profile of v3, /device:TPU:1, one launch (start us, length us, event | category | flops | bytes accessed | tf_op | source)
XLA Modules:
  0.0 38.5 jit_solution(2371072083508701904)
XLA Ops:
  0.6 36.3 %shard_map.77 = (bf16[128,4096]{1,0:T(8,128)(2,1)S(1)}, f32[1,2752]{1,0:T(1,128)S(1)}) custom-call(s32[1,8]{1,0:T(1,128)} %bitcast.9, bf16[128,4096]{1,0:T(8,128)(2,1)} %bitcast.6, bf16[128,4096]{1,0:T(8,128)(2,1)} %top_hbm.1, bf16[128,128]{1,0:T(8,128)(2,1)} %bitcast.8, bf16[4096,128]{1,0:T(8,128)(2,1)} %bitcast.7, f32[1,4096]{1,0:T(1,128)} %g_hbm.1), custom_call_target="tpu_custom_call" | custom-call | tf_op jit(solution)/shard_map/pallas_call | solution.py:491
  36.9 1.0 %copy.10 = bf16[1,128,4096]{2,1,0:T(8,128)(2,1)} copy(bf16[1,128,4096]{2,1,0:T(8,128)(2,1)S(1)} %bitcast.5) | data formatting | bytes 2097152
  37.9 0.6 %copy.11 = f32[1,2752]{1,0:T(1,128)} copy(f32[1,2752]{1,0:T(1,128)S(1)} %get-tuple-element.9) | data formatting | bytes 22016

commit v4 on v3

--- a/solution.py
+++ b/solution.py
@@ -443,8 +443,10 @@
     for i in range(len(GROUPS)):
         chain(i + 1)
         pl.when(lead)(lambda i=i: y_sum(i))
+    late_start = lead & (sec == 0) & (dp == 0)
+    pl.when(late_start)(z_sum)
     chain(len(GROUPS) + 1)
-    pl.when(lead)(z_sum)
+    pl.when(lead & jnp.logical_not(late_start))(z_sum)
     pl.when(core == 1)(twin_last)
 
     @pl.when(lead)

time: 38.7 us -> 38.2 us (0.987)
  Pallas kernels: 36.3 us -> 35.9 us
    pallas_call x1, Pallas kernels: 36.3 us -> 35.9 us  [shards(): pl.pallas_call(kernel, out_shape=(jax.ShapeDtypeStruct(wide, BF16), jax.S...]
where the time goes in v4:
time: 38.2 us; the launch traced here: 38.1 us
  Pallas kernels  35.9 us (94%)
  local copies, waits for them, and re-layouts  1.57 us (4%)
  between operations  0.64 us (2%)
    pallas_call x1, Pallas kernels, shards(): pl.pallas_call(kernel, out_shape=(jax.ShapeDtypeStruct(wide, BF16), jax.S...  35.9 us
    unnamed x2, local copies, waits for them, and re-layouts  1.57 us

profile of v4, /device:TPU:1, one launch (start us, length us, event | category | flops | bytes accessed | tf_op | source)
XLA Modules:
  0.0 38.1 jit_solution(5658705209531819608)
XLA Ops:
  0.6 35.9 %shard_map.77 = (bf16[128,4096]{1,0:T(8,128)(2,1)S(1)}, f32[1,2752]{1,0:T(1,128)S(1)}) custom-call(s32[1,8]{1,0:T(1,128)} %bitcast.9, bf16[128,4096]{1,0:T(8,128)(2,1)} %bitcast.6, bf16[128,4096]{1,0:T(8,128)(2,1)} %top_hbm.1, bf16[128,128]{1,0:T(8,128)(2,1)} %bitcast.8, bf16[4096,128]{1,0:T(8,128)(2,1)} %bitcast.7, f32[1,4096]{1,0:T(1,128)} %g_hbm.1), custom_call_target="tpu_custom_call" | custom-call | tf_op jit(solution)/shard_map/pallas_call | solution.py:493
  36.5 1.0 %copy.10 = bf16[1,128,4096]{2,1,0:T(8,128)(2,1)} copy(bf16[1,128,4096]{2,1,0:T(8,128)(2,1)S(1)} %bitcast.5) | data formatting | bytes 2097152
  37.5 0.6 %copy.11 = f32[1,2752]{1,0:T(1,128)} copy(f32[1,2752]{1,0:T(1,128)S(1)} %get-tuple-element.9) | data formatting | bytes 22016
